TPU v7x, 256 devices: a whole 4x4x8 slice. The times are simulated.
256 devices in a mesh: slab: 16 (over y, x), mode: 16 (over z, core).
Axes of the slice: x: 4, y: 4, z: 8, core: 2. Of those that a mesh axis runs over, the one named last changes fastest.
Arguments:
- tensor: bfloat16 [512, 131072], P('mode', 'slab'), may hold values from -24 to 24, as said below
- start_block: float32 [512, 128], replicated, may hold values from -6 to 6
Outputs:
- basis_rows: float32 [512, 128], P('mode')
- core_coeffs: float32 [131072, 128], P(('slab', 'mode'))
Inputs may be any that keep to these rules, and one draw needn't show every extreme that they name: `tensor`: entries of the unfolding; each is a row factor times a column factor times a bounded random term.
All inputs are finite; a program needn't handle non-finite values.
Results may differ from a plain program's by a relative error of at most 0.0029.
Values may be sent and summed in bfloat16 or wider, within the bound.
A program may use at most 64 MiB of HBM per device.

v0:
```python
import jax
import jax.numpy as jnp
from jax import lax
from jax.sharding import PartitionSpec as P

highest = lax.Precision.HIGHEST
contract_cols = (((1,), (1,)), ((), ()))
contract_rows = (((0,), (0,)), ((), ()))


def orthonormal(image_block):
    small_gram = jnp.dot(image_block.T, image_block, precision=highest)
    factor = jnp.linalg.cholesky(small_gram)
    return lax.linalg.triangular_solve(
        factor, image_block, left_side=False, lower=True, transpose_a=True
    )


def shards(tensor, start_block):
    row_count = tensor.shape[0]
    mode_index = lax.axis_index("mode")
    regrouped = lax.all_to_all(tensor, "mode", split_axis=1, concat_axis=0, tiled=True)
    local_gram = lax.dot_general(
        regrouped, regrouped, contract_cols, preferred_element_type=jnp.float32
    )
    gram_total = lax.psum(local_gram, ("slab", "mode"))
    image_block = jnp.dot(gram_total, start_block, precision=highest)
    basis_full = orthonormal(image_block)
    basis_low = basis_full.astype(jnp.bfloat16)
    basis_rows = lax.dynamic_slice_in_dim(basis_full, mode_index * row_count, row_count, 0)
    core_coeffs = lax.dot_general(
        regrouped, basis_low, contract_rows, preferred_element_type=jnp.float32
    )
    return (basis_rows, core_coeffs)


def solution(mesh):
    placed = (P("mode", "slab"), P())
    return jax.shard_map(
        shards,
        mesh=mesh,
        in_specs=placed,
        out_specs=(P("mode", None), P(("slab", "mode"), None)),
        check_vma=False,
    )
```

profile of v0, /device:TPU:1, one launch (start us, length us, event | category | flops | bytes accessed | tf_op | source)
XLA Modules:
  0.0 325.9 jit_solution(6227881989262356702)
XLA Ops:
  7.2 0.0 copy-start
  7.2 0.0 all-reduce.2.cloned.1.call-start
  7.2 1.1 copy.16
  8.4 27.0 %all_to_all.19 = bf16[32,16,512]{2,0,1:T(8,128)(2,1)S(1)} all-to-all(bf16[32,16,512]{2,0,1:T(8,128)(2,1)S(1)} %bitcast.28), channel_id=1, replica_groups=mesh['slab'=16,'mode'=16] {'mode'}, dimensions={1} | all-to-all | bytes 1048576 | tf_op jit(solution)/shard_map/all_to_all | solution.py:22
  35.3 1.5 fusion.5
  36.8 0.0 all-reduce.2.cloned.1.call-update
  36.9 254.3 %all-reduce.2.cloned.1.call-done = f32[512,512]{1,0:T(8,128)} async-done(((f32[512,512]{1,0:T(8,128)}), f32[512,512]{1,0:T(8,128)}) %all-reduce.2.cloned.1.call-update) | async-done | bytes 1048592 | tf_op jit(solution)/shard_map/psum | solution.py:26
  291.2 0.0 copy-done
  291.2 2.2 fusion.6
  293.4 0.6 fusion.7
  294.0 0.1 copy.12
  294.1 11.7 %cholesky.16 = f32[128,128]{1,0:T(8,128)S(1)} custom-call(f32[128,128]{1,0:T(8,128)S(1)} %fusion.4), custom_call_target="Cholesky" | custom-call | tf_op jit(solution)/shard_map/jit(cholesky)/cholesky | solution.py:13
  305.8 0.6 compare_reduce_fusion
  306.5 0.7 fusion.1
  307.1 9.8 %custom-call.6 = f32[1,128,128]{1,2,0:T(8,128)S(1)} custom-call(f32[1,128,128]{2,1,0:T(8,128)S(1)} %fusion.1), custom_call_target="InvertDiagBlocksLowerTriangular" | custom-call | tf_op jit(solution)/shard_map/triangular_solve | solution.py:14
  317.0 0.4 fusion.2
  317.3 0.3 convolution_bitcast_fusion
  317.6 0.6 constant_dynamic-slice_fusion
  318.2 0.8 copy.13
  (2 shorter events, 0.0 us)
Async XLA Ops:
  7.2 284.0 %copy-start = (f32[512,128]{1,0:T(8,128)S(1)}, f32[512,128]{1,0:T(8,128)}, u32[]{:S(2)}) copy-start(f32[512,128]{1,0:T(8,128)} %param.3) | copy-start | bytes 786436
  7.2 284.0 %all-reduce.2.cloned.1.call-start = ((), (), s32[]{:S(2)}) async-start(), calls=%async_computation.1 | async-start | bytes 2097152 | tf_op jit(solution)/shard_map/psum | solution.py:26
Sparse Core Ops, SparseCore 0:
  37.0 254.1 all-reduce.1
where the time goes:
time: 327 us; the launch traced here: 326 us
  waiting for transfers between devices  254 us (78%)
  blocking collectives  27 us (8%)
  other arithmetic  22.9 us (7%)
  between operations  14.1 us (4%)
  matrix products  4.92 us (2%)
    psum x1, waiting for transfers between devices, shards(): gram_total = lax.psum(local_gram, ('slab', 'mode'))  254 us
    all_to_all x1, blocking collectives, shards(): lax.all_to_all(tensor, 'mode', split_axis=1, concat_axis=0, tiled=True)  27 us
    another operation x3, other arithmetic, orthonormal(): factor = jnp.linalg.cholesky(small_gram)  12.4 us
    another operation x2, other arithmetic, orthonormal(): lax.linalg.triangular_solve(factor, image_block, left_side=False, lower=T...  10.5 us
  transfers between devices with their start and end apart: 1, of which 1 were waited for; matrix products, arithmetic and copies ran while one was open for 0% of the time, Pallas kernels for 0%

commit v1 on v0

v1 whole, which is shorter than its diff:
```python
import functools

import jax
import jax.numpy as jnp
from jax import lax
from jax.experimental import pallas as pl
from jax.experimental.pallas import tpu as pltpu
from jax.sharding import PartitionSpec as P

MESH = pl.DeviceIdType.MESH
highest = lax.Precision.HIGHEST
BF16, F32 = jnp.bfloat16, jnp.float32


def exchange(sizes, tensor_ref, start_ref, regrouped_out, image_ref,
             regrouped, split_start, partial_low, plane_in, z_in, mine,
             own_sem, out_sem, a2a_send, a2a_recv, rs_send, rs_recv,
             z_send, z_recv, ag_send, ag_recv):
    slabs, modes = sizes
    chips_z, plane = modes // 2, slabs * 2
    rows, block = tensor_ref.shape[0], regrouped.shape[1]
    piece = plane_in.shape[1]
    slab, mode = lax.axis_index("slab"), lax.axis_index("mode")
    z, core = mode // 2, lax.rem(mode, 2)
    spot = slab * 2 + core

    def z_peer(dz, flip):
        peer_core = core if flip == 0 else 1 - core
        return lax.rem(z + dz + chips_z, chips_z) * 2 + peer_core

    def plane_peer(ds, flip):
        peer_core = core if flip == 0 else 1 - core
        return lax.rem(slab + ds + slabs, slabs), peer_core

    half = chips_z // 2
    order = [half]
    for distance in range(half - 1, 0, -1):
        order += [distance, -distance]
    z_steps = [(dz, flip) for dz in order for flip in (0, 1)] + [(0, 1)]
    plane_steps = [(ds, flip) for ds in range(1, slabs) for flip in (0, 1)] + [(0, 1)]

    barrier = pltpu.get_barrier_semaphore()
    for dz, flip in z_steps:
        pl.semaphore_signal(barrier, inc=1, device_id=(slab, z_peer(dz, flip)), device_id_type=MESH)
    for ds, flip in plane_steps[:-1]:
        other, peer_core = plane_peer(ds, flip)
        pl.semaphore_signal(barrier, inc=1, device_id=(other, z * 2 + peer_core), device_id_type=MESH)
    own = pltpu.make_async_copy(
        tensor_ref.at[:, pl.ds(pl.multiple_of(mode * block, block), block)],
        regrouped.at[pl.ds(pl.multiple_of(mode * rows, rows), rows), :],
        own_sem,
    )
    own.start()
    pl.semaphore_wait(barrier, len(z_steps) + len(plane_steps) - 1)

    def a2a(index, dz, flip, landing):
        peer = z_peer(dz, flip)
        return pltpu.make_async_remote_copy(
            src_ref=tensor_ref.at[:, pl.ds(pl.multiple_of(peer * block, block), block)],
            dst_ref=regrouped.at[pl.ds(pl.multiple_of(landing * rows, rows), rows), :],
            send_sem=a2a_send.at[index],
            recv_sem=a2a_recv.at[index],
            device_id=(slab, peer),
            device_id_type=MESH,
        )

    for index, (dz, flip) in enumerate(z_steps):
        a2a(index, dz, flip, mode).start()

    start_t = start_ref[...].T
    high = start_t.astype(BF16)
    split_start[0] = high
    split_start[1] = (start_t - high.astype(F32)).astype(BF16)

    own.wait()
    for index, (dz, flip) in enumerate(z_steps):
        a2a(index, dz, flip, z_peer(-dz, flip)).wait_recv()

    out = pltpu.make_async_copy(regrouped, regrouped_out, out_sem)
    out.start()
    whole = regrouped[...]
    projected = jnp.dot(split_start[0], whole, preferred_element_type=F32)
    projected += jnp.dot(split_start[1], whole, preferred_element_type=F32)
    high = projected.astype(BF16)
    low = (projected - high.astype(F32)).astype(BF16)
    last = (((1,), (1,)), ((), ()))
    partial = lax.dot_general(whole, high, last, preferred_element_type=F32)
    partial += lax.dot_general(whole, low, last, preferred_element_type=F32)
    partial_low[...] = partial.astype(BF16).reshape(partial_low.shape)

    def scatter(index, ds, flip, landing):
        other, peer_core = plane_peer(ds, flip)
        return pltpu.make_async_remote_copy(
            src_ref=partial_low.at[other * 2 + peer_core],
            dst_ref=plane_in.at[landing],
            send_sem=rs_send.at[index],
            recv_sem=rs_recv.at[index],
            device_id=(other, z * 2 + peer_core),
            device_id_type=MESH,
        )

    for index, (ds, flip) in enumerate(plane_steps):
        scatter(index, ds, flip, spot).start()
    plane_in[spot] = partial_low[spot]
    for index, (ds, flip) in enumerate(plane_steps):
        other, peer_core = plane_peer(-ds, flip)
        scatter(index, ds, flip, other * 2 + peer_core).wait_recv()
    mine[...] = jnp.sum(plane_in[...].astype(F32), axis=0)
    z_in[z] = mine[...]

    def along_z(index, dz, landing):
        peer = z_peer(dz, 0)
        return pltpu.make_async_remote_copy(
            src_ref=mine,
            dst_ref=z_in.at[landing],
            send_sem=z_send.at[index],
            recv_sem=z_recv.at[index],
            device_id=(slab, peer),
            device_id_type=MESH,
        )

    for index, dz in enumerate(order):
        along_z(index, dz, z).start()
    for index, dz in enumerate(order):
        along_z(index, dz, lax.rem(z - dz + chips_z, chips_z)).wait_recv()
    image_ref[spot] = jnp.sum(z_in[...], axis=0)

    def gather(index, ds, flip, landing):
        other, peer_core = plane_peer(ds, flip)
        return pltpu.make_async_remote_copy(
            src_ref=image_ref.at[spot],
            dst_ref=image_ref.at[landing],
            send_sem=ag_send.at[index],
            recv_sem=ag_recv.at[index],
            device_id=(other, z * 2 + peer_core),
            device_id_type=MESH,
        )

    for index, (ds, flip) in enumerate(plane_steps):
        gather(index, ds, flip, spot).start()
    for index, (ds, flip) in enumerate(plane_steps):
        other, peer_core = plane_peer(-ds, flip)
        gather(index, ds, flip, other * 2 + peer_core).wait_recv()

    for index, (dz, flip) in enumerate(z_steps):
        a2a(index, dz, flip, mode).wait_send()
    for index, (ds, flip) in enumerate(plane_steps):
        scatter(index, ds, flip, spot).wait_send()
        gather(index, ds, flip, spot).wait_send()
    for index, dz in enumerate(order):
        along_z(index, dz, z).wait_send()
    out.wait()


def orthonormal(image_block):
    small_gram = jnp.dot(image_block.T, image_block, precision=highest)
    factor = jnp.linalg.cholesky(small_gram)
    return lax.linalg.triangular_solve(
        factor, image_block, left_side=False, lower=True, transpose_a=True
    )


def shards(sizes, tensor, start_block):
    slabs, modes = sizes
    rows, width = tensor.shape
    full, rank = start_block.shape
    block = width // modes
    plane = slabs * 2
    piece = full // plane
    dma = pltpu.SemaphoreType.DMA
    regrouped, image = pl.pallas_call(
        functools.partial(exchange, sizes),
        out_shape=(
            jax.ShapeDtypeStruct((full, block), BF16),
            jax.ShapeDtypeStruct((plane, piece, rank), F32),
        ),
        in_specs=[pl.BlockSpec(memory_space=pl.ANY), pl.BlockSpec(memory_space=pltpu.VMEM)],
        out_specs=(pl.BlockSpec(memory_space=pl.ANY), pl.BlockSpec(memory_space=pltpu.VMEM)),
        scratch_shapes=[
            pltpu.VMEM((full, block), BF16),
            pltpu.VMEM((2, rank, full), BF16),
            pltpu.VMEM((plane, piece, rank), BF16),
            pltpu.VMEM((plane, piece, rank), BF16),
            pltpu.VMEM((modes // 2, piece, rank), F32),
            pltpu.VMEM((piece, rank), F32),
            dma, dma,
            dma((modes,)), dma((modes,)),
            dma((plane,)), dma((plane,)),
            dma((modes // 2,)), dma((modes // 2,)),
            dma((plane,)), dma((plane,)),
        ],
        compiler_params=pltpu.CompilerParams(collective_id=0, has_side_effects=True),
        name="exchange",
    )(tensor, start_block)
    basis_full = orthonormal(image.reshape(full, rank))
    basis_low = basis_full.astype(BF16)
    basis_rows = lax.dynamic_slice_in_dim(basis_full, lax.axis_index("mode") * rows, rows, 0)
    core_coeffs = lax.dot_general(
        regrouped, basis_low, (((0,), (0,)), ((), ())), preferred_element_type=F32
    )
    return (basis_rows, core_coeffs)


def solution(mesh):
    sizes = (mesh.shape["slab"], mesh.shape["mode"])
    return jax.shard_map(
        functools.partial(shards, sizes),
        mesh=mesh,
        in_specs=(P("mode", "slab"), P()),
        out_specs=(P("mode", None), P(("slab", "mode"), None)),
        check_vma=False,
    )
```

time: 327 us -> 70.9 us (0.22)
  waiting for transfers between devices: 254 us -> 0 us
  Pallas kernels: 0 us -> 43.5 us
  blocking collectives: 27 us -> 0 us
  between operations: 14.1 us -> 0.71 us
    psum x1 -> x0, waiting for transfers between devices: 254 us -> none  [shards(): gram_total = lax.psum(local_gram, ('slab', 'mode'))]
    pallas_call x0 -> x1, Pallas kernels: none -> 43.5 us  [shards(): pl.pallas_call(functools.partial(exchange, sizes), out_shape=(jax.ShapeDt...]
    all_to_all x1 -> x0, blocking collectives: 27 us -> none  [shards(): lax.all_to_all(tensor, 'mode', split_axis=1, concat_axis=0, tiled=True)]
  transfers between devices with their start and end apart: 1 -> 0, of which waited for: 1 -> 0; matrix products, arithmetic and copies ran while one was open for 0% -> 0% of each run, Pallas kernels for 0% -> 0%
where the time goes in v1:
time: 70.9 us; the launch traced here: 70.8 us
  Pallas kernels  43.5 us (61%)
  other arithmetic  22.9 us (32%)
  matrix products  3.02 us (4%)
  local copies, waits for them, and re-layouts  0.71 us (1%)
  between operations  0.71 us (1%)
    pallas_call x1, Pallas kernels, shards(): pl.pallas_call(functools.partial(exchange, sizes), out_shape=(jax.ShapeDt...  43.5 us
    another operation x3, other arithmetic, orthonormal(): factor = jnp.linalg.cholesky(small_gram)  12.4 us
    another operation x2, other arithmetic, orthonormal(): lax.linalg.triangular_solve(factor, image_block, left_side=False, lower=T...  10.5 us
    dot_general x1, matrix products, orthonormal(): small_gram = jnp.dot(image_block.T, image_block, precision=highest)  1.62 us

profile of v1, /device:TPU:1, one launch (start us, length us, event | category | flops | bytes accessed | tf_op | source)
XLA Modules:
  0.0 70.8 jit_solution(12551831483969144798)
XLA Ops:
  0.6 43.5 %exchange.1 = (bf16[512,512]{1,0:T(8,128)(2,1)}, f32[32,16,128]{2,1,0:T(8,128)}) custom-call(bf16[32,8192]{1,0:T(8,128)(2,1)} %tensor_ref.1, f32[512,128]{1,0:T(8,128)} %start_ref.1), custom_call_target="tpu_custom_call" | custom-call | tf_op jit(solution)/shard_map/exchange/pallas_call | solution.py:171
  44.1 1.6 %convolution_bitcast_fusion = f32[128,128]{1,0:T(8,128)S(1)} fusion(f32[32,16,128]{2,1,0:T(8,128)} %get-tuple-element.4), kind=kOutput, calls=%fused_computation | convolution fusion | flops 100663296 | bytes 327680 | tf_op jit(solution)/shard_map/dot_general | solution.py:156
  45.7 0.0 copy-start.1
  45.7 0.1 copy.6
  45.8 0.0 copy-start
  45.8 11.7 %cholesky.16 = f32[128,128]{1,0:T(8,128)S(1)} custom-call(f32[128,128]{1,0:T(8,128)S(1)} %fusion.5), custom_call_target="Cholesky" | custom-call | tf_op jit(solution)/shard_map/jit(cholesky)/cholesky | solution.py:157
  57.6 0.6 compare_reduce_fusion
  58.2 0.7 fusion.2
  58.9 9.8 %custom-call.6 = f32[1,128,128]{1,2,0:T(8,128)S(1)} custom-call(f32[1,128,128]{2,1,0:T(8,128)S(1)} %fusion.2), custom_call_target="InvertDiagBlocksLowerTriangular" | custom-call | tf_op jit(solution)/shard_map/triangular_solve | solution.py:158
  68.7 0.0 copy-done.1
  68.7 0.4 fusion.3
  69.1 0.6 constant_dynamic-slice_fusion
  69.7 0.0 copy-done
  69.7 1.0 %fusion = f32[512,128]{1,0:T(8,128)} fusion(bf16[512,512]{1,0:T(8,128)(2,1)S(1)} %copy-done, f32[512,128]{1,0:T(8,128)S(1)} %fusion.3), kind=kOutput, calls=%fused_computation.1 | convolution fusion | flops 67174400 | bytes 1048576 | tf_op jit(solution)/shard_map/dot_general | solution.py:198
  (2 shorter events, 0.0 us)
Async XLA Ops:
  45.7 23.0 %copy-start.1 = (f32[32,16,128]{2,1,0:T(8,128)S(1)}, f32[32,16,128]{2,1,0:T(8,128)}, u32[]{:S(2)}) copy-start(f32[32,16,128]{2,1,0:T(8,128)} %get-tuple-element.4) | copy-start | bytes 786436
  45.8 23.9 %copy-start = (bf16[512,512]{1,0:T(8,128)(2,1)S(1)}, bf16[512,512]{1,0:T(8,128)(2,1)}, u32[]{:S(2)}) copy-start(bf16[512,512]{1,0:T(8,128)(2,1)} %get-tuple-element.5) | copy-start | bytes 1572868

commit v2 on v1

--- a/solution.py
+++ b/solution.py
@@ -152,11 +152,72 @@
     out.wait()
 
 
-def orthonormal(image_block):
-    small_gram = jnp.dot(image_block.T, image_block, precision=highest)
-    factor = jnp.linalg.cholesky(small_gram)
-    return lax.linalg.triangular_solve(
-        factor, image_block, left_side=False, lower=True, transpose_a=True
+def inverse_factor(gram):
+    n = gram.shape[0]
+    tall = n // 8
+    lane = lax.broadcasted_iota(jnp.int32, (8, n), 1)
+    sub = lax.broadcasted_iota(jnp.int32, (8, n), 0)
+    spread = lambda x, k: jnp.broadcast_to(x[:, k : k + 1], (8, n))
+    pick = lambda x, k: jnp.broadcast_to(x[k : k + 1], (8, n))
+    work = [gram[8 * r : 8 * r + 8, :] for r in range(tall)]
+    out = []
+    ahead = [spread(work[0], k) for k in range(8)]
+    for p in range(tall):
+        below = range(p, tall)
+        cols = [{r: ahead[k] if r == p else spread(work[r], 8 * p + k) for r in below} for k in range(8)]
+        if p + 1 < tall:
+            ahead = [spread(work[p + 1], 8 * (p + 1) + k) for k in range(8)]
+        done = jnp.zeros((8, n), F32)
+        for s in range(0, 8, 2):
+            j = 8 * p + s
+            col_a, col_b = cols[s], cols[s + 1]
+            a, b, c = pick(col_a[p], s), pick(col_a[p], s + 1), pick(col_b[p], s + 1)
+            det = a * c - b * b
+            inv = 1.0 / det
+            ia, ib, ic = c * inv, b * inv, a * inv
+            for k in range(s + 2, 8):
+                va, vb = pick(col_a[p], k), pick(col_b[p], k)
+                ta, tb = ia * va - ib * vb, ic * vb - ib * va
+                for r in below:
+                    cols[k][r] = cols[k][r] - (col_a[r] * ta + col_b[r] * tb)
+            if p + 1 < tall:
+                for k in range(8):
+                    va, vb = pick(col_a[p + 1], k), pick(col_b[p + 1], k)
+                    ta, tb = ia * va - ib * vb, ic * vb - ib * va
+                    ahead[k] = ahead[k] - (col_a[p + 1] * ta + col_b[p + 1] * tb)
+            row_a, row_b = pick(work[p], s), pick(work[p], s + 1)
+            unit_a = jnp.where(lane == j, 1.0, 0.0).astype(F32)
+            unit_b = jnp.where(lane == j + 1, 1.0, 0.0).astype(F32)
+            full_a, full_b = row_a + unit_a, row_b + unit_b
+            ta = ia * full_a - ib * full_b
+            tb = ic * full_b - ib * full_a
+            left_a = jnp.where(lane < j, row_a, unit_a)
+            left_b = jnp.where(lane < j, row_b, unit_b)
+            root_a = lax.rsqrt(a)
+            root_b = lax.rsqrt(det * (root_a * root_a))
+            w_a = left_a * root_a
+            w_b = (left_b - (b * root_a) * w_a) * root_b
+            done = jnp.where(sub == s, w_a, jnp.where(sub == s + 1, w_b, done))
+            for r in below:
+                work[r] = work[r] - (col_a[r] * ta + col_b[r] * tb)
+        out.append(done)
+    return jnp.concatenate(out, axis=0)
+
+
+def finish(regrouped_ref, image_ref, rows_ref, core_ref, basis):
+    image = image_ref[...].reshape(basis.shape)
+    image = image * lax.rsqrt(jnp.sum(image * image, axis=0, keepdims=True))
+    across = (((0,), (0,)), ((), ()))
+    gram = lax.dot_general(image, image, across, precision=highest, preferred_element_type=F32)
+    inverse = inverse_factor(gram)
+    whole = lax.dot_general(
+        image, inverse, (((1,), (1,)), ((), ())), precision=highest, preferred_element_type=F32
+    )
+    basis[...] = whole
+    count = rows_ref.shape[0]
+    rows_ref[...] = basis[pl.ds(pl.multiple_of(lax.axis_index("mode") * count, count), count), :]
+    core_ref[...] = lax.dot_general(
+        regrouped_ref[...], whole.astype(BF16), across, preferred_element_type=F32
     )
 
 
@@ -192,13 +253,15 @@
         compiler_params=pltpu.CompilerParams(collective_id=0, has_side_effects=True),
         name="exchange",
     )(tensor, start_block)
-    basis_full = orthonormal(image.reshape(full, rank))
-    basis_low = basis_full.astype(BF16)
-    basis_rows = lax.dynamic_slice_in_dim(basis_full, lax.axis_index("mode") * rows, rows, 0)
-    core_coeffs = lax.dot_general(
-        regrouped, basis_low, (((0,), (0,)), ((), ())), preferred_element_type=F32
-    )
-    return (basis_rows, core_coeffs)
+    return pl.pallas_call(
+        finish,
+        out_shape=(
+            jax.ShapeDtypeStruct((rows, rank), F32),
+            jax.ShapeDtypeStruct((block, rank), F32),
+        ),
+        scratch_shapes=[pltpu.VMEM((full, rank), F32)],
+        name="finish",
+    )(regrouped, image)
 
 
 def solution(mesh):

time: 70.9 us -> 50.8 us (0.72)
  other arithmetic: 22.9 us -> 0 us
  Pallas kernels: 43.5 us -> 50 us
  matrix products: 3.02 us -> 0 us
  local copies, waits for them, and re-layouts: 0.71 us -> 0 us
    another operation x5 -> x0, other arithmetic: 22.9 us -> none  [the longest x3 12.4 us: orthonormal(): factor = jnp.linalg.cholesky(small_gram)]
    pallas_call x0 -> x1, Pallas kernels: none -> 6.57 us  [shards(): pl.pallas_call(finish, out_shape=(jax.ShapeDtypeStruct((rows, rank), F32)...]
    dot_general x2 -> x0, matrix products: 2.66 us -> none  [the longest x1 1.62 us: orthonormal(): small_gram = jnp.dot(image_block.T, image_block, precision=highest)]
where the time goes in v2:
time: 50.8 us; the launch traced here: 50.7 us
  Pallas kernels  50 us (98%)
  between operations  0.64 us (1%)
    pallas_call x1, Pallas kernels, shards(): pl.pallas_call(functools.partial(exchange, sizes), out_shape=(jax.ShapeDt...  43.4 us
    pallas_call x1, Pallas kernels, shards(): pl.pallas_call(finish, out_shape=(jax.ShapeDtypeStruct((rows, rank), F32)...  6.57 us

profile of v2, /device:TPU:1, one launch (start us, length us, event | category | flops | bytes accessed | tf_op | source)
XLA Modules:
  0.0 50.7 jit_solution(7782994836990037807)
XLA Ops:
  0.6 43.4 %exchange.1 = (bf16[512,512]{1,0:T(8,128)(2,1)}, f32[32,16,128]{2,1,0:T(8,128)}) custom-call(bf16[32,8192]{1,0:T(8,128)(2,1)} %tensor_ref.1, f32[512,128]{1,0:T(8,128)} %start_ref.1), custom_call_target="tpu_custom_call" | custom-call | tf_op jit(solution)/shard_map/exchange/pallas_call | solution.py:232
  44.1 6.6 %finish.1 = (f32[32,128]{1,0:T(8,128)}, f32[512,128]{1,0:T(8,128)}) custom-call(bf16[512,512]{1,0:T(8,128)(2,1)} %get-tuple-element.4.regrouped_ref, f32[32,16,128]{2,1,0:T(8,128)} %get-tuple-element.5.image_ref), custom_call_target="tpu_custom_call" | custom-call | tf_op jit(solution)/shard_map/finish/pallas_call | solution.py:256

commit v3 on v2

--- a/solution.py
+++ b/solution.py
@@ -12,9 +12,9 @@
 BF16, F32 = jnp.bfloat16, jnp.float32
 
 
-def exchange(sizes, tensor_ref, start_ref, regrouped_out, image_ref,
+def exchange(sizes, tensor_ref, start_ref, turned_ref, image_ref,
              regrouped, split_start, partial_low, plane_in, z_in, mine,
-             own_sem, out_sem, a2a_send, a2a_recv, rs_send, rs_recv,
+             own_sem, z_known, x_known, core_known, y_known, a2a_send, a2a_recv, rs_send, rs_recv,
              z_send, z_recv, ag_send, ag_recv):
     slabs, modes = sizes
     chips_z, plane = modes // 2, slabs * 2
@@ -39,19 +39,31 @@
     z_steps = [(dz, flip) for dz in order for flip in (0, 1)] + [(0, 1)]
     plane_steps = [(ds, flip) for ds in range(1, slabs) for flip in (0, 1)] + [(0, 1)]
 
+    side = 4
+    x, y = lax.rem(slab, side), slab // side
+    x_beside = [(y * side + lax.rem(x + d, side), mode) for d in (1, side - 1)]
+    y_beside = [(lax.rem(y + d, side) * side + x, mode) for d in (1, side - 1)]
+    z_beside = [(slab, z_peer(dz, 0)) for dz in (1, -1)]
+    other_core = (slab, z_peer(0, 1))
+
+    def tell(semaphore, device):
+        pl.semaphore_signal(semaphore, inc=1, device_id=device, device_id_type=MESH)
+
     barrier = pltpu.get_barrier_semaphore()
-    for dz, flip in z_steps:
-        pl.semaphore_signal(barrier, inc=1, device_id=(slab, z_peer(dz, flip)), device_id_type=MESH)
-    for ds, flip in plane_steps[:-1]:
-        other, peer_core = plane_peer(ds, flip)
-        pl.semaphore_signal(barrier, inc=1, device_id=(other, z * 2 + peer_core), device_id_type=MESH)
+    beside = z_beside + [(slab, z_peer(dz, 1)) for dz in (1, -1)] + [other_core] + x_beside + y_beside
+    for device in beside:
+        tell(barrier, device)
     own = pltpu.make_async_copy(
         tensor_ref.at[:, pl.ds(pl.multiple_of(mode * block, block), block)],
         regrouped.at[pl.ds(pl.multiple_of(mode * rows, rows), rows), :],
         own_sem,
     )
     own.start()
-    pl.semaphore_wait(barrier, len(z_steps) + len(plane_steps) - 1)
+    start_t = start_ref[...].T
+    high = start_t.astype(BF16)
+    split_start[0] = high
+    split_start[1] = (start_t - high.astype(F32)).astype(BF16)
+    pl.semaphore_wait(barrier, len(beside))
 
     def a2a(index, dz, flip, landing):
         peer = z_peer(dz, flip)
@@ -64,20 +76,41 @@
             device_id_type=MESH,
         )
 
-    for index, (dz, flip) in enumerate(z_steps):
-        a2a(index, dz, flip, mode).start()
-
-    start_t = start_ref[...].T
-    high = start_t.astype(BF16)
-    split_start[0] = high
-    split_start[1] = (start_t - high.astype(F32)).astype(BF16)
+    def send(distances):
+        for index, (dz, flip) in enumerate(z_steps):
+            if dz in distances:
+                a2a(index, dz, flip, mode).start()
+
+    def reach(known, devices):
+        for way in (0, 1):
+            tell(known.at[way], devices[way])
+
+    def heard(known):
+        for way in (0, 1):
+            pl.semaphore_wait(known.at[way], 1)
+
+    reach(z_known.at[0], z_beside)
+    reach(x_known, x_beside)
+    send((1, -1, 0))
+    for further in range(1, half):
+        heard(z_known.at[further - 1])
+        if further + 1 < half:
+            reach(z_known.at[further], z_beside)
+        if further == 1:
+            send((2, -2))
+    send([dz for dz in order if abs(dz) > 2])
+    heard(x_known)
+    tell(core_known, other_core)
+    pl.semaphore_wait(core_known, 1)
+    reach(y_known.at[0], y_beside)
+    heard(y_known.at[0])
+    reach(y_known.at[1], y_beside)
+    heard(y_known.at[1])
 
     own.wait()
     for index, (dz, flip) in enumerate(z_steps):
         a2a(index, dz, flip, z_peer(-dz, flip)).wait_recv()
 
-    out = pltpu.make_async_copy(regrouped, regrouped_out, out_sem)
-    out.start()
     whole = regrouped[...]
     projected = jnp.dot(split_start[0], whole, preferred_element_type=F32)
     projected += jnp.dot(split_start[1], whole, preferred_element_type=F32)
@@ -102,6 +135,7 @@
     for index, (ds, flip) in enumerate(plane_steps):
         scatter(index, ds, flip, spot).start()
     plane_in[spot] = partial_low[spot]
+    turned_ref[...] = regrouped[...].T
     for index, (ds, flip) in enumerate(plane_steps):
         other, peer_core = plane_peer(-ds, flip)
         scatter(index, ds, flip, other * 2 + peer_core).wait_recv()
@@ -149,7 +183,6 @@
         gather(index, ds, flip, spot).wait_send()
     for index, dz in enumerate(order):
         along_z(index, dz, z).wait_send()
-    out.wait()
 
 
 def inverse_factor(gram):
@@ -204,7 +237,7 @@
     return jnp.concatenate(out, axis=0)
 
 
-def finish(regrouped_ref, image_ref, rows_ref, core_ref, basis):
+def finish(turned_ref, image_ref, rows_ref, core_ref, basis):
     image = image_ref[...].reshape(basis.shape)
     image = image * lax.rsqrt(jnp.sum(image * image, axis=0, keepdims=True))
     across = (((0,), (0,)), ((), ()))
@@ -216,9 +249,7 @@
     basis[...] = whole
     count = rows_ref.shape[0]
     rows_ref[...] = basis[pl.ds(pl.multiple_of(lax.axis_index("mode") * count, count), count), :]
-    core_ref[...] = lax.dot_general(
-        regrouped_ref[...], whole.astype(BF16), across, preferred_element_type=F32
-    )
+    core_ref[...] = jnp.dot(turned_ref[...], whole.astype(BF16), preferred_element_type=F32)
 
 
 def shards(sizes, tensor, start_block):
@@ -228,15 +259,15 @@
     block = width // modes
     plane = slabs * 2
     piece = full // plane
-    dma = pltpu.SemaphoreType.DMA
-    regrouped, image = pl.pallas_call(
+    dma, regular = pltpu.SemaphoreType.DMA, pltpu.SemaphoreType.REGULAR
+    turned, image = pl.pallas_call(
         functools.partial(exchange, sizes),
         out_shape=(
-            jax.ShapeDtypeStruct((full, block), BF16),
-            jax.ShapeDtypeStruct((plane, piece, rank), F32),
+            pltpu.VMEM((block, full), BF16),
+            pltpu.VMEM((plane, piece, rank), F32),
         ),
         in_specs=[pl.BlockSpec(memory_space=pl.ANY), pl.BlockSpec(memory_space=pltpu.VMEM)],
-        out_specs=(pl.BlockSpec(memory_space=pl.ANY), pl.BlockSpec(memory_space=pltpu.VMEM)),
+        out_specs=(pl.BlockSpec(memory_space=pltpu.VMEM), pl.BlockSpec(memory_space=pltpu.VMEM)),
         scratch_shapes=[
             pltpu.VMEM((full, block), BF16),
             pltpu.VMEM((2, rank, full), BF16),
@@ -244,7 +275,8 @@
             pltpu.VMEM((plane, piece, rank), BF16),
             pltpu.VMEM((modes // 2, piece, rank), F32),
             pltpu.VMEM((piece, rank), F32),
-            dma, dma,
+            dma,
+            regular((modes // 4 - 1, 2)), regular((2,)), regular, regular((2, 2)),
             dma((modes,)), dma((modes,)),
             dma((plane,)), dma((plane,)),
             dma((modes // 2,)), dma((modes // 2,)),
@@ -259,9 +291,10 @@
             jax.ShapeDtypeStruct((rows, rank), F32),
             jax.ShapeDtypeStruct((block, rank), F32),
         ),
+        in_specs=[pl.BlockSpec(memory_space=pltpu.VMEM)] * 2,
         scratch_shapes=[pltpu.VMEM((full, rank), F32)],
         name="finish",
-    )(regrouped, image)
+    )(*(pltpu.with_memory_space_constraint(x, pltpu.VMEM) for x in (turned, image)))
 
 
 def solution(mesh):

time: 50.8 us -> 47.6 us (0.937)
  Pallas kernels: 50 us -> 46.8 us
    pallas_call x1, Pallas kernels: 43.4 us -> 41.4 us  [shards(): pl.pallas_call(functools.partial(exchange, sizes), out_shape=(pltpu.VMEM(...]
    pallas_call x1, Pallas kernels: 6.57 us -> 5.43 us  [shards(): pl.pallas_call(finish, out_shape=(jax.ShapeDtypeStruct((rows, rank), F32)...]
where the time goes in v3:
time: 47.6 us; the launch traced here: 47.5 us
  Pallas kernels  46.8 us (98%)
  between operations  0.64 us (1%)
    pallas_call x1, Pallas kernels, shards(): pl.pallas_call(functools.partial(exchange, sizes), out_shape=(pltpu.VMEM(...  41.4 us
    pallas_call x1, Pallas kernels, shards(): pl.pallas_call(finish, out_shape=(jax.ShapeDtypeStruct((rows, rank), F32)...  5.43 us

profile of v3, /device:TPU:1, one launch (start us, length us, event | category | flops | bytes accessed | tf_op | source)
XLA Modules:
  0.0 47.5 jit_solution(2407687090469773070)
XLA Ops:
  0.6 41.4 %exchange.1 = (bf16[512,512]{1,0:T(8,128)(2,1)S(1)}, f32[32,16,128]{2,1,0:T(8,128)S(1)}) custom-call(bf16[32,8192]{1,0:T(8,128)(2,1)} %tensor_ref.1, f32[512,128]{1,0:T(8,128)} %start_ref.1), custom_call_target="tpu_custom_call" | custom-call | tf_op jit(solution)/shard_map/exchange/pallas_call | solution.py:263
  42.0 5.4 %finish.1 = (f32[32,128]{1,0:T(8,128)}, f32[512,128]{1,0:T(8,128)}) custom-call(bf16[512,512]{1,0:T(8,128)(2,1)S(1)} %get-tuple-element.4.turned_ref, f32[32,16,128]{2,1,0:T(8,128)S(1)} %get-tuple-element.5.image_ref), custom_call_target="tpu_custom_call" | custom-call | tf_op jit(solution)/shard_map/finish/pallas_call | solution.py:288

commit v4 on v3

--- a/solution.py
+++ b/solution.py
@@ -13,8 +13,8 @@
 
 
 def exchange(sizes, tensor_ref, start_ref, turned_ref, image_ref,
-             regrouped, split_start, partial_low, plane_in, z_in, mine,
-             own_sem, z_known, x_known, core_known, y_known, a2a_send, a2a_recv, rs_send, rs_recv,
+             start, regrouped, split_start, partial_low, plane_in, z_in, mine,
+             start_sem, own_sem, z_known, x_known, core_known, y_known, a2a_send, a2a_recv, rs_send, rs_recv,
              z_send, z_recv, ag_send, ag_recv):
     slabs, modes = sizes
     chips_z, plane = modes // 2, slabs * 2
@@ -28,19 +28,25 @@
         peer_core = core if flip == 0 else 1 - core
         return lax.rem(z + dz + chips_z, chips_z) * 2 + peer_core
 
-    def plane_peer(ds, flip):
-        peer_core = core if flip == 0 else 1 - core
-        return lax.rem(slab + ds + slabs, slabs), peer_core
+    def plane_peer(offset, sign=1):
+        dy, dx, flip = offset
+        row = lax.rem(slab // 4 + sign * dy + 4, 4)
+        column = lax.rem(lax.rem(slab, 4) + sign * dx + 4, 4)
+        return row * 4 + column, core if flip == 0 else 1 - core
 
     half = chips_z // 2
     order = [half]
     for distance in range(half - 1, 0, -1):
         order += [distance, -distance]
     z_steps = [(dz, flip) for dz in order for flip in (0, 1)] + [(0, 1)]
-    plane_steps = [(ds, flip) for ds in range(1, slabs) for flip in (0, 1)] + [(0, 1)]
-
     side = 4
     x, y = lax.rem(slab, side), slab // side
+
+    def hops(offset):
+        return sum(min(d, side - d) for d in offset[:2])
+
+    plane_steps = [(dy, dx, flip) for dy in range(side) for dx in range(side) for flip in (0, 1)][1:]
+    plane_steps.sort(key=lambda offset: -hops(offset))
     x_beside = [(y * side + lax.rem(x + d, side), mode) for d in (1, side - 1)]
     y_beside = [(lax.rem(y + d, side) * side + x, mode) for d in (1, side - 1)]
     z_beside = [(slab, z_peer(dz, 0)) for dz in (1, -1)]
@@ -59,10 +65,8 @@
         own_sem,
     )
     own.start()
-    start_t = start_ref[...].T
-    high = start_t.astype(BF16)
-    split_start[0] = high
-    split_start[1] = (start_t - high.astype(F32)).astype(BF16)
+    fetch = pltpu.make_async_copy(start_ref, start, start_sem)
+    fetch.start()
     pl.semaphore_wait(barrier, len(beside))
 
     def a2a(index, dz, flip, landing):
@@ -107,6 +111,12 @@
     reach(y_known.at[1], y_beside)
     heard(y_known.at[1])
 
+    fetch.wait()
+    start_t = start[...].T
+    high = start_t.astype(BF16)
+    split_start[0] = high
+    split_start[1] = (start_t - high.astype(F32)).astype(BF16)
+
     own.wait()
     for index, (dz, flip) in enumerate(z_steps):
         a2a(index, dz, flip, z_peer(-dz, flip)).wait_recv()
@@ -121,8 +131,8 @@
     partial += lax.dot_general(whole, low, last, preferred_element_type=F32)
     partial_low[...] = partial.astype(BF16).reshape(partial_low.shape)
 
-    def scatter(index, ds, flip, landing):
-        other, peer_core = plane_peer(ds, flip)
+    def scatter(index, offset, landing):
+        other, peer_core = plane_peer(offset)
         return pltpu.make_async_remote_copy(
             src_ref=partial_low.at[other * 2 + peer_core],
             dst_ref=plane_in.at[landing],
@@ -132,13 +142,13 @@
             device_id_type=MESH,
         )
 
-    for index, (ds, flip) in enumerate(plane_steps):
-        scatter(index, ds, flip, spot).start()
+    for index, offset in enumerate(plane_steps):
+        scatter(index, offset, spot).start()
     plane_in[spot] = partial_low[spot]
     turned_ref[...] = regrouped[...].T
-    for index, (ds, flip) in enumerate(plane_steps):
-        other, peer_core = plane_peer(-ds, flip)
-        scatter(index, ds, flip, other * 2 + peer_core).wait_recv()
+    for index, offset in enumerate(plane_steps):
+        other, peer_core = plane_peer(offset, -1)
+        scatter(index, offset, other * 2 + peer_core).wait_recv()
     mine[...] = jnp.sum(plane_in[...].astype(F32), axis=0)
     z_in[z] = mine[...]
 
@@ -159,8 +169,8 @@
         along_z(index, dz, lax.rem(z - dz + chips_z, chips_z)).wait_recv()
     image_ref[spot] = jnp.sum(z_in[...], axis=0)
 
-    def gather(index, ds, flip, landing):
-        other, peer_core = plane_peer(ds, flip)
+    def gather(index, offset, landing):
+        other, peer_core = plane_peer(offset)
         return pltpu.make_async_remote_copy(
             src_ref=image_ref.at[spot],
             dst_ref=image_ref.at[landing],
@@ -170,17 +180,17 @@
             device_id_type=MESH,
         )
 
-    for index, (ds, flip) in enumerate(plane_steps):
-        gather(index, ds, flip, spot).start()
-    for index, (ds, flip) in enumerate(plane_steps):
-        other, peer_core = plane_peer(-ds, flip)
-        gather(index, ds, flip, other * 2 + peer_core).wait_recv()
+    for index, offset in enumerate(plane_steps):
+        gather(index, offset, spot).start()
+    for index, offset in enumerate(plane_steps):
+        other, peer_core = plane_peer(offset, -1)
+        gather(index, offset, other * 2 + peer_core).wait_recv()
 
     for index, (dz, flip) in enumerate(z_steps):
         a2a(index, dz, flip, mode).wait_send()
-    for index, (ds, flip) in enumerate(plane_steps):
-        scatter(index, ds, flip, spot).wait_send()
-        gather(index, ds, flip, spot).wait_send()
+    for index, offset in enumerate(plane_steps):
+        scatter(index, offset, spot).wait_send()
+        gather(index, offset, spot).wait_send()
     for index, dz in enumerate(order):
         along_z(index, dz, z).wait_send()
 
@@ -266,16 +276,17 @@
             pltpu.VMEM((block, full), BF16),
             pltpu.VMEM((plane, piece, rank), F32),
         ),
-        in_specs=[pl.BlockSpec(memory_space=pl.ANY), pl.BlockSpec(memory_space=pltpu.VMEM)],
+        in_specs=[pl.BlockSpec(memory_space=pl.ANY)] * 2,
         out_specs=(pl.BlockSpec(memory_space=pltpu.VMEM), pl.BlockSpec(memory_space=pltpu.VMEM)),
         scratch_shapes=[
+            pltpu.VMEM((full, rank), F32),
             pltpu.VMEM((full, block), BF16),
             pltpu.VMEM((2, rank, full), BF16),
             pltpu.VMEM((plane, piece, rank), BF16),
             pltpu.VMEM((plane, piece, rank), BF16),
             pltpu.VMEM((modes // 2, piece, rank), F32),
             pltpu.VMEM((piece, rank), F32),
-            dma,
+            dma, dma,
             regular((modes // 4 - 1, 2)), regular((2,)), regular, regular((2, 2)),
             dma((modes,)), dma((modes,)),
             dma((plane,)), dma((plane,)),

time: 47.6 us -> 46.1 us (0.968)
  Pallas kernels: 46.8 us -> 45.4 us
    pallas_call x1, Pallas kernels: 41.4 us -> 40 us  [shards(): pl.pallas_call(functools.partial(exchange, sizes), out_shape=(pltpu.VMEM(...]
where the time goes in v4:
time: 46.1 us; the launch traced here: 46 us
  Pallas kernels  45.4 us (98%)
  between operations  0.64 us (1%)
    pallas_call x1, Pallas kernels, shards(): pl.pallas_call(functools.partial(exchange, sizes), out_shape=(pltpu.VMEM(...  40 us
    pallas_call x1, Pallas kernels, shards(): pl.pallas_call(finish, out_shape=(jax.ShapeDtypeStruct((rows, rank), F32)...  5.42 us

profile of v4, /device:TPU:1, one launch (start us, length us, event | category | flops | bytes accessed | tf_op | source)
XLA Modules:
  0.0 46.0 jit_solution(18181782687150160474)
XLA Ops:
  0.6 40.0 %exchange.1 = (bf16[512,512]{1,0:T(8,128)(2,1)S(1)}, f32[32,16,128]{2,1,0:T(8,128)S(1)}) custom-call(bf16[32,8192]{1,0:T(8,128)(2,1)} %tensor_ref.1, f32[512,128]{1,0:T(8,128)} %start_ref.1), custom_call_target="tpu_custom_call" | custom-call | tf_op jit(solution)/shard_map/exchange/pallas_call | solution.py:273
  40.6 5.4 %finish.1 = (f32[32,128]{1,0:T(8,128)}, f32[512,128]{1,0:T(8,128)}) custom-call(bf16[512,512]{1,0:T(8,128)(2,1)S(1)} %get-tuple-element.4.turned_ref, f32[32,16,128]{2,1,0:T(8,128)S(1)} %get-tuple-element.5.image_ref), custom_call_target="tpu_custom_call" | custom-call | tf_op jit(solution)/shard_map/finish/pallas_call | solution.py:299

commit v5 on v4

--- a/solution.py
+++ b/solution.py
@@ -114,21 +114,23 @@
     fetch.wait()
     start_t = start[...].T
     high = start_t.astype(BF16)
-    split_start[0] = high
-    split_start[1] = (start_t - high.astype(F32)).astype(BF16)
+    rank = start.shape[1]
+    split_start[:rank, :] = high
+    split_start[rank:, :] = (start_t - high.astype(F32)).astype(BF16)
 
     own.wait()
     for index, (dz, flip) in enumerate(z_steps):
         a2a(index, dz, flip, z_peer(-dz, flip)).wait_recv()
 
     whole = regrouped[...]
-    projected = jnp.dot(split_start[0], whole, preferred_element_type=F32)
-    projected += jnp.dot(split_start[1], whole, preferred_element_type=F32)
+    halves = jnp.dot(split_start[...], whole, preferred_element_type=F32)
+    projected = halves[:rank] + halves[rank:]
     high = projected.astype(BF16)
     low = (projected - high.astype(F32)).astype(BF16)
-    last = (((1,), (1,)), ((), ()))
-    partial = lax.dot_general(whole, high, last, preferred_element_type=F32)
-    partial += lax.dot_general(whole, low, last, preferred_element_type=F32)
+    halves = lax.dot_general(
+        whole, jnp.concatenate([high, low], axis=0), (((1,), (1,)), ((), ())), preferred_element_type=F32
+    )
+    partial = halves[:, :rank] + halves[:, rank:]
     partial_low[...] = partial.astype(BF16).reshape(partial_low.shape)
 
     def scatter(index, offset, landing):
@@ -203,37 +205,35 @@
     spread = lambda x, k: jnp.broadcast_to(x[:, k : k + 1], (8, n))
     pick = lambda x, k: jnp.broadcast_to(x[k : k + 1], (8, n))
     work = [gram[8 * r : 8 * r + 8, :] for r in range(tall)]
+    nothing = work[0] * 0.0
+    ahead = [spread(work[0], k) + nothing for k in range(8)]
     out = []
-    ahead = [spread(work[0], k) for k in range(8)]
     for p in range(tall):
-        below = range(p, tall)
-        cols = [{r: ahead[k] if r == p else spread(work[r], 8 * p + k) for r in below} for k in range(8)]
-        if p + 1 < tall:
+        cols, more = ahead, p + 1 < tall
+        far = {r: [spread(work[r], 8 * p + k) for k in range(8)] for r in range(p + 1, tall)}
+        if more:
+            beside = [x + nothing for x in far[p + 1]]
             ahead = [spread(work[p + 1], 8 * (p + 1) + k) for k in range(8)]
-        done = jnp.zeros((8, n), F32)
+        rows = work[p]
+        done = nothing
         for s in range(0, 8, 2):
             j = 8 * p + s
             col_a, col_b = cols[s], cols[s + 1]
-            a, b, c = pick(col_a[p], s), pick(col_a[p], s + 1), pick(col_b[p], s + 1)
+            a, b, c = pick(col_a, s), pick(col_a, s + 1), pick(col_b, s + 1)
             det = a * c - b * b
             inv = 1.0 / det
             ia, ib, ic = c * inv, b * inv, a * inv
-            for k in range(s + 2, 8):
-                va, vb = pick(col_a[p], k), pick(col_b[p], k)
-                ta, tb = ia * va - ib * vb, ic * vb - ib * va
-                for r in below:
-                    cols[k][r] = cols[k][r] - (col_a[r] * ta + col_b[r] * tb)
-            if p + 1 < tall:
+            mul_a, mul_b = ia * col_a - ib * col_b, ic * col_b - ib * col_a
+            if more:
+                next_a, next_b = beside[s], beside[s + 1]
+                low_a, low_b = ia * next_a - ib * next_b, ic * next_b - ib * next_a
                 for k in range(8):
-                    va, vb = pick(col_a[p + 1], k), pick(col_b[p + 1], k)
-                    ta, tb = ia * va - ib * vb, ic * vb - ib * va
-                    ahead[k] = ahead[k] - (col_a[p + 1] * ta + col_b[p + 1] * tb)
-            row_a, row_b = pick(work[p], s), pick(work[p], s + 1)
+                    ahead[k] = ahead[k] - (low_a * pick(next_a, k) + low_b * pick(next_b, k))
+                for k in range(s + 2, 8):
+                    beside[k] = beside[k] - (low_a * pick(cols[k], s) + low_b * pick(cols[k], s + 1))
+            row_a, row_b = pick(rows, s), pick(rows, s + 1)
             unit_a = jnp.where(lane == j, 1.0, 0.0).astype(F32)
             unit_b = jnp.where(lane == j + 1, 1.0, 0.0).astype(F32)
-            full_a, full_b = row_a + unit_a, row_b + unit_b
-            ta = ia * full_a - ib * full_b
-            tb = ic * full_b - ib * full_a
             left_a = jnp.where(lane < j, row_a, unit_a)
             left_b = jnp.where(lane < j, row_b, unit_b)
             root_a = lax.rsqrt(a)
@@ -241,9 +241,29 @@
             w_a = left_a * root_a
             w_b = (left_b - (b * root_a) * w_a) * root_b
             done = jnp.where(sub == s, w_a, jnp.where(sub == s + 1, w_b, done))
-            for r in below:
-                work[r] = work[r] - (col_a[r] * ta + col_b[r] * tb)
+            if s < 6:
+                rows = jnp.where((lane == j) | (lane == j + 1), 0.0, rows) - (mul_a * left_a + mul_b * left_b)
+            swept_a = jnp.where(sub == s, 1.0 - ia, jnp.where(sub == s + 1, ib, mul_a))
+            swept_b = jnp.where(sub == s, ib, jnp.where(sub == s + 1, 1.0 - ic, mul_b))
+            for k in range(8):
+                if k < s or (k > s + 1):
+                    if more or k > s + 1:
+                        cols[k] = cols[k] - (swept_a * pick(cols[k], s) + swept_b * pick(cols[k], s + 1))
+            cols[s] = jnp.where(sub == s, 1.0, 0.0) - swept_a
+            cols[s + 1] = jnp.where(sub == s + 1, 1.0, 0.0) - swept_b
         out.append(done)
+        if more:
+            within = (lane >= 8 * p) & (lane < 8 * p + 8)
+            terms = [
+                cols[k] * jnp.where(within, jnp.where(lane == 8 * p + k, 1.0, 0.0), pick(work[p], k))
+                for k in range(8)
+            ]
+            solved = ((terms[0] + terms[1]) + (terms[2] + terms[3])) + ((terms[4] + terms[5]) + (terms[6] + terms[7]))
+            against = [pick(solved, k) for k in range(8)]
+            for r in range(p + 1, tall):
+                terms = [far[r][k] * against[k] for k in range(8)]
+                total = ((terms[0] + terms[1]) + (terms[2] + terms[3])) + ((terms[4] + terms[5]) + (terms[6] + terms[7]))
+                work[r] = jnp.where(within, 0.0, work[r]) - total
     return jnp.concatenate(out, axis=0)
 
 
@@ -281,7 +301,7 @@
         scratch_shapes=[
             pltpu.VMEM((full, rank), F32),
             pltpu.VMEM((full, block), BF16),
-            pltpu.VMEM((2, rank, full), BF16),
+            pltpu.VMEM((2 * rank, full), BF16),
             pltpu.VMEM((plane, piece, rank), BF16),
             pltpu.VMEM((plane, piece, rank), BF16),
             pltpu.VMEM((modes // 2, piece, rank), F32),

time: 46.1 us -> 45.2 us (0.980)
  Pallas kernels: 45.4 us -> 44.5 us
    pallas_call x1, Pallas kernels: 5.42 us -> 4.62 us  [shards(): pl.pallas_call(finish, out_shape=(jax.ShapeDtypeStruct((rows, rank), F32)...]
where the time goes in v5:
time: 45.2 us; the launch traced here: 45.1 us
  Pallas kernels  44.5 us (98%)
  between operations  0.64 us (1%)
    pallas_call x1, Pallas kernels, shards(): pl.pallas_call(functools.partial(exchange, sizes), out_shape=(pltpu.VMEM(...  39.9 us
    pallas_call x1, Pallas kernels, shards(): pl.pallas_call(finish, out_shape=(jax.ShapeDtypeStruct((rows, rank), F32)...  4.62 us

profile of v5, /device:TPU:1, one launch (start us, length us, event | category | flops | bytes accessed | tf_op | source)
XLA Modules:
  0.0 45.1 jit_solution(17713556515900265384)
XLA Ops:
  0.6 39.9 %exchange.1 = (bf16[512,512]{1,0:T(8,128)(2,1)S(1)}, f32[32,16,128]{2,1,0:T(8,128)S(1)}) custom-call(bf16[32,8192]{1,0:T(8,128)(2,1)} %tensor_ref.1, f32[512,128]{1,0:T(8,128)} %start_ref.1), custom_call_target="tpu_custom_call" | custom-call | tf_op jit(solution)/shard_map/exchange/pallas_call | solution.py:293
  40.5 4.6 %finish.1 = (f32[32,128]{1,0:T(8,128)}, f32[512,128]{1,0:T(8,128)}) custom-call(bf16[512,512]{1,0:T(8,128)(2,1)S(1)} %get-tuple-element.4.turned_ref, f32[32,16,128]{2,1,0:T(8,128)S(1)} %get-tuple-element.5.image_ref), custom_call_target="tpu_custom_call" | custom-call | tf_op jit(solution)/shard_map/finish/pallas_call | solution.py:319

commit v6 on v5

--- a/solution.py
+++ b/solution.py
@@ -123,15 +123,25 @@
         a2a(index, dz, flip, z_peer(-dz, flip)).wait_recv()
 
     whole = regrouped[...]
-    halves = jnp.dot(split_start[...], whole, preferred_element_type=F32)
-    projected = halves[:rank] + halves[rank:]
+    half = whole.shape[1] // 2
+    projected = []
+    for columns in (whole[:, :half], whole[:, half:]):
+        halves = jnp.dot(split_start[...], columns, preferred_element_type=F32)
+        projected.append(halves[:rank] + halves[rank:])
+    projected = jnp.concatenate(projected, axis=1)
     high = projected.astype(BF16)
     low = (projected - high.astype(F32)).astype(BF16)
-    halves = lax.dot_general(
-        whole, jnp.concatenate([high, low], axis=0), (((1,), (1,)), ((), ())), preferred_element_type=F32
-    )
-    partial = halves[:, :rank] + halves[:, rank:]
-    partial_low[...] = partial.astype(BF16).reshape(partial_low.shape)
+    both = jnp.concatenate([high, low], axis=0)
+    share = whole.shape[0] // 2
+    for part in range(2):
+        halves = lax.dot_general(
+            whole[part * share : (part + 1) * share], both, (((1,), (1,)), ((), ())), preferred_element_type=F32
+        )
+        partial = halves[:, :rank] + halves[:, rank:]
+        pieces = partial_low.shape[0] // 2
+        partial_low[part * pieces : (part + 1) * pieces] = partial.astype(BF16).reshape(
+            (pieces,) + partial_low.shape[1:]
+        )
 
     def scatter(index, offset, landing):
         other, peer_core = plane_peer(offset)
@@ -148,7 +158,9 @@
         scatter(index, offset, spot).start()
     plane_in[spot] = partial_low[spot]
     turned_ref[...] = regrouped[...].T
-    for index, offset in enumerate(plane_steps):
+    for index, (dz, flip) in enumerate(z_steps):
+        a2a(index, dz, flip, mode).wait_send()
+    for index, offset in reversed(list(enumerate(plane_steps))):
         other, peer_core = plane_peer(offset, -1)
         scatter(index, offset, other * 2 + peer_core).wait_recv()
     mine[...] = jnp.sum(plane_in[...].astype(F32), axis=0)
@@ -167,7 +179,9 @@
 
     for index, dz in enumerate(order):
         along_z(index, dz, z).start()
-    for index, dz in enumerate(order):
+    for index, offset in enumerate(plane_steps):
+        scatter(index, offset, spot).wait_send()
+    for index, dz in reversed(list(enumerate(order))):
         along_z(index, dz, lax.rem(z - dz + chips_z, chips_z)).wait_recv()
     image_ref[spot] = jnp.sum(z_in[...], axis=0)
 
@@ -184,17 +198,13 @@
 
     for index, offset in enumerate(plane_steps):
         gather(index, offset, spot).start()
+    for index, dz in enumerate(order):
+        along_z(index, dz, z).wait_send()
     for index, offset in enumerate(plane_steps):
+        gather(index, offset, spot).wait_send()
+    for index, offset in reversed(list(enumerate(plane_steps))):
         other, peer_core = plane_peer(offset, -1)
         gather(index, offset, other * 2 + peer_core).wait_recv()
-
-    for index, (dz, flip) in enumerate(z_steps):
-        a2a(index, dz, flip, mode).wait_send()
-    for index, offset in enumerate(plane_steps):
-        scatter(index, offset, spot).wait_send()
-        gather(index, offset, spot).wait_send()
-    for index, dz in enumerate(order):
-        along_z(index, dz, z).wait_send()
 
 
 def inverse_factor(gram):
@@ -271,10 +281,20 @@
     image = image_ref[...].reshape(basis.shape)
     image = image * lax.rsqrt(jnp.sum(image * image, axis=0, keepdims=True))
     across = (((0,), (0,)), ((), ()))
-    gram = lax.dot_general(image, image, across, precision=highest, preferred_element_type=F32)
+    half = image.shape[0] // 2
+    gram = sum(
+        lax.dot_general(rows, rows, across, precision=highest, preferred_element_type=F32)
+        for rows in (image[:half], image[half:])
+    )
     inverse = inverse_factor(gram)
-    whole = lax.dot_general(
-        image, inverse, (((1,), (1,)), ((), ())), precision=highest, preferred_element_type=F32
+    whole = jnp.concatenate(
+        [
+            lax.dot_general(
+                rows, inverse, (((1,), (1,)), ((), ())), precision=highest, preferred_element_type=F32
+            )
+            for rows in (image[:half], image[half:])
+        ],
+        axis=0,
     )
     basis[...] = whole
     count = rows_ref.shape[0]

time: 45.2 us -> 44.8 us (level)
  no operation moved by 1% of the time
where the time goes in v6:
time: 44.8 us; the launch traced here: 44.7 us
  Pallas kernels  44.1 us (98%)
  between operations  0.64 us (1%)
    pallas_call x1, Pallas kernels, shards(): pl.pallas_call(functools.partial(exchange, sizes), out_shape=(pltpu.VMEM(...  39.6 us
    pallas_call x1, Pallas kernels, shards(): pl.pallas_call(finish, out_shape=(jax.ShapeDtypeStruct((rows, rank), F32)...  4.42 us

profile of v6, /device:TPU:1, one launch (start us, length us, event | category | flops | bytes accessed | tf_op | source)
XLA Modules:
  0.0 44.7 jit_solution(13811111919454410609)
XLA Ops:
  0.6 39.6 %exchange.1 = (bf16[512,512]{1,0:T(8,128)(2,1)S(1)}, f32[32,16,128]{2,1,0:T(8,128)S(1)}) custom-call(bf16[32,8192]{1,0:T(8,128)(2,1)} %tensor_ref.1, f32[512,128]{1,0:T(8,128)} %start_ref.1), custom_call_target="tpu_custom_call" | custom-call | tf_op jit(solution)/shard_map/exchange/pallas_call | solution.py:313
  40.3 4.4 %finish.1 = (f32[32,128]{1,0:T(8,128)}, f32[512,128]{1,0:T(8,128)}) custom-call(bf16[512,512]{1,0:T(8,128)(2,1)S(1)} %get-tuple-element.4.turned_ref, f32[32,16,128]{2,1,0:T(8,128)S(1)} %get-tuple-element.5.image_ref), custom_call_target="tpu_custom_call" | custom-call | tf_op jit(solution)/shard_map/finish/pallas_call | solution.py:339

commit v7 on v6

--- a/solution.py
+++ b/solution.py
@@ -69,8 +69,15 @@
     fetch.start()
     pl.semaphore_wait(barrier, len(beside))
 
+    def target(dz, flip):
+        return z_peer(dz * (1 - 2 * core), flip)
+
+    def source(dz, flip):
+        sender = core if flip == 0 else 1 - core
+        return z_peer(-dz * (1 - 2 * sender), flip)
+
     def a2a(index, dz, flip, landing):
-        peer = z_peer(dz, flip)
+        peer = target(dz, flip)
         return pltpu.make_async_remote_copy(
             src_ref=tensor_ref.at[:, pl.ds(pl.multiple_of(peer * block, block), block)],
             dst_ref=regrouped.at[pl.ds(pl.multiple_of(landing * rows, rows), rows), :],
@@ -120,7 +127,7 @@
 
     own.wait()
     for index, (dz, flip) in enumerate(z_steps):
-        a2a(index, dz, flip, z_peer(-dz, flip)).wait_recv()
+        a2a(index, dz, flip, source(dz, flip)).wait_recv()
 
     whole = regrouped[...]
     half = whole.shape[1] // 2
@@ -167,7 +174,7 @@
     z_in[z] = mine[...]
 
     def along_z(index, dz, landing):
-        peer = z_peer(dz, 0)
+        peer = target(dz, 0)
         return pltpu.make_async_remote_copy(
             src_ref=mine,
             dst_ref=z_in.at[landing],
@@ -182,7 +189,7 @@
     for index, offset in enumerate(plane_steps):
         scatter(index, offset, spot).wait_send()
     for index, dz in reversed(list(enumerate(order))):
-        along_z(index, dz, lax.rem(z - dz + chips_z, chips_z)).wait_recv()
+        along_z(index, dz, source(dz, 0) // 2).wait_recv()
     image_ref[spot] = jnp.sum(z_in[...], axis=0)
 
     def gather(index, offset, landing):

time: 44.8 us -> 44.8 us (level)
  no operation moved by 1% of the time
where the time goes in v7:
time: 44.8 us; the launch traced here: 44.7 us
  Pallas kernels  44.1 us (98%)
  between operations  0.64 us (1%)
    pallas_call x1, Pallas kernels, shards(): pl.pallas_call(functools.partial(exchange, sizes), out_shape=(pltpu.VMEM(...  39.6 us
    pallas_call x1, Pallas kernels, shards(): pl.pallas_call(finish, out_shape=(jax.ShapeDtypeStruct((rows, rank), F32)...  4.42 us

profile of v7, /device:TPU:1, one launch (start us, length us, event | category | flops | bytes accessed | tf_op | source)
XLA Modules:
  0.0 44.7 jit_solution(12403448381475581415)
XLA Ops:
  0.6 39.6 %exchange.1 = (bf16[512,512]{1,0:T(8,128)(2,1)S(1)}, f32[32,16,128]{2,1,0:T(8,128)S(1)}) custom-call(bf16[32,8192]{1,0:T(8,128)(2,1)} %tensor_ref.1, f32[512,128]{1,0:T(8,128)} %start_ref.1), custom_call_target="tpu_custom_call" | custom-call | tf_op jit(solution)/shard_map/exchange/pallas_call | solution.py:320
  40.3 4.4 %finish.1 = (f32[32,128]{1,0:T(8,128)}, f32[512,128]{1,0:T(8,128)}) custom-call(bf16[512,512]{1,0:T(8,128)(2,1)S(1)} %get-tuple-element.4.turned_ref, f32[32,16,128]{2,1,0:T(8,128)S(1)} %get-tuple-element.5.image_ref), custom_call_target="tpu_custom_call" | custom-call | tf_op jit(solution)/shard_map/finish/pallas_call | solution.py:346

commit v8 on v7

--- a/solution.py
+++ b/solution.py
@@ -294,15 +294,19 @@
         for rows in (image[:half], image[half:])
     )
     inverse = inverse_factor(gram)
-    whole = jnp.concatenate(
-        [
-            lax.dot_general(
-                rows, inverse, (((1,), (1,)), ((), ())), precision=highest, preferred_element_type=F32
-            )
-            for rows in (image[:half], image[half:])
-        ],
-        axis=0,
-    )
+    turned_inverse = inverse.T
+    inverse_high = turned_inverse.astype(BF16)
+    inverse_low = (turned_inverse - inverse_high.astype(F32)).astype(BF16)
+    both = jnp.concatenate([inverse_high, inverse_low], axis=1)
+    rank = image.shape[1]
+    image_high = image.astype(BF16)
+    image_low = (image - image_high.astype(F32)).astype(BF16)
+    whole = []
+    for part in (slice(0, half), slice(half, None)):
+        halves = jnp.dot(image_high[part], both, preferred_element_type=F32)
+        lower = jnp.dot(image_low[part], inverse_high, preferred_element_type=F32)
+        whole.append(halves[:, :rank] + (halves[:, rank:] + lower))
+    whole = jnp.concatenate(whole, axis=0)
     basis[...] = whole
     count = rows_ref.shape[0]
     rows_ref[...] = basis[pl.ds(pl.multiple_of(lax.axis_index("mode") * count, count), count), :]

time: 44.8 us -> 44.8 us (level)
  no operation moved by 1% of the time
where the time goes in v8:
time: 44.8 us; the launch traced here: 44.7 us
  Pallas kernels  44.1 us (98%)
  between operations  0.64 us (1%)
    pallas_call x1, Pallas kernels, shards(): pl.pallas_call(functools.partial(exchange, sizes), out_shape=(pltpu.VMEM(...  39.6 us
    pallas_call x1, Pallas kernels, shards(): pl.pallas_call(finish, out_shape=(jax.ShapeDtypeStruct((rows, rank), F32)...  4.42 us

profile of v8, /device:TPU:1, one launch (start us, length us, event | category | flops | bytes accessed | tf_op | source)
XLA Modules:
  0.0 44.7 jit_solution(14864862598179378560)
XLA Ops:
  0.6 39.6 %exchange.1 = (bf16[512,512]{1,0:T(8,128)(2,1)S(1)}, f32[32,16,128]{2,1,0:T(8,128)S(1)}) custom-call(bf16[32,8192]{1,0:T(8,128)(2,1)} %tensor_ref.1, f32[512,128]{1,0:T(8,128)} %start_ref.1), custom_call_target="tpu_custom_call" | custom-call | tf_op jit(solution)/shard_map/exchange/pallas_call | solution.py:324
  40.3 4.4 %finish.1 = (f32[32,128]{1,0:T(8,128)}, f32[512,128]{1,0:T(8,128)}) custom-call(bf16[512,512]{1,0:T(8,128)(2,1)S(1)} %get-tuple-element.4.turned_ref, f32[32,16,128]{2,1,0:T(8,128)S(1)} %get-tuple-element.5.image_ref), custom_call_target="tpu_custom_call" | custom-call | tf_op jit(solution)/shard_map/finish/pallas_call | solution.py:350
